TPU v7x, 128 devices: a whole 4x4x4 slice. The times are simulated.
128 devices in a mesh: row: 16 (over z_lo, y, core), col: 8 (over z_hi, x).
Axes of the slice: x: 4, y: 4, z: 4 (z_hi: 2, z_lo: 2; z = z_hi * 2 + z_lo), core: 2. Of those that a mesh axis runs over, the one named last changes fastest.
Arguments:
- activations: bfloat16 [3072, 16384], P(('row', 'col')), may hold values from -14 to 14
- tenant_ids: int32 [3072], P(('row', 'col')), may hold values from 0 to 63
- concept_labels: int32 [3072], P(('row', 'col')), may hold values from 0 to 1
Outputs:
- covariance: float32 [16384, 16384], P('row', 'col')
- cross: float32 [128, 16384], P(None, ('row', 'col'))
All inputs are finite; a program needn't handle non-finite values.
Results may differ from a plain program's by a relative error of at most 0.0003.
Values may be sent and summed in bfloat16 or wider, within the bound.
A program may use at most 128 MiB of HBM per device.

v0:
```python
import jax
import jax.numpy as jnp
from jax import lax
from jax.sharding import PartitionSpec as P

TENANTS = 64
LABELS = 2


def shards(activations, tenant_ids, concept_labels):
    local_tokens = activations.shape[0]
    width = activations.shape[1]
    row_count = lax.axis_size("row")
    col_count = lax.axis_size("col")
    groups = TENANTS * LABELS
    codes = tenant_ids * LABELS + concept_labels
    codes_rows = lax.all_gather(codes, "row", axis=0, tiled=True)
    row_piece = lax.all_to_all(activations, "row", split_axis=1, concat_axis=0, tiled=True)
    row_panel, codes_all = (
        lax.all_gather(row_piece, "col", axis=0, tiled=True),
        lax.all_gather(codes_rows, "col", axis=0, tiled=True),
    )
    total = row_panel.shape[0]
    row_width = row_panel.shape[1]
    row_view = row_panel.reshape(col_count, row_count, local_tokens, row_width)
    col_piece = lax.all_to_all(activations, "col", split_axis=1, concat_axis=0, tiled=True)
    col_panel = lax.all_gather(col_piece, "row", axis=0, tiled=True)
    col_view = col_panel.reshape(row_count, col_count, local_tokens, col_panel.shape[1])
    gram = jnp.einsum("abtf,batg->fg", row_view, col_view, preferred_element_type=jnp.float32)
    mean_row = jnp.sum(row_panel, axis=0, dtype=jnp.float32) / total
    mean_col = jnp.sum(col_panel, axis=0, dtype=jnp.float32) / total
    covariance = gram / total - mean_row[:, None] * mean_col[None, :]
    slice_width = width // (row_count * col_count)
    slice_start = lax.axis_index("col") * slice_width
    mean_slice = lax.dynamic_slice_in_dim(mean_row, slice_start, slice_width)
    group_ids = jnp.arange(groups, dtype=jnp.int32)
    onehot_all = codes_all[:, None] == group_ids[None, :]
    counts = jnp.sum(onehot_all.astype(jnp.float32), axis=0)
    panel_slice = lax.dynamic_slice_in_dim(row_panel, slice_start, slice_width, 1)
    sums = lax.dot_general(
        onehot_all.astype(jnp.bfloat16),
        panel_slice,
        (((0,), (0,)), ((), ())),
        preferred_element_type=jnp.float32,
    )
    cross = groups / total * (sums - counts[:, None] * mean_slice[None, :])
    return (covariance, cross)


def solution(mesh):
    placed = (P(("row", "col"), None), P(("row", "col")), P(("row", "col")))
    return jax.shard_map(
        shards,
        mesh=mesh,
        in_specs=placed,
        out_specs=(P("row", "col"), P(None, ("row", "col"))),
        check_vma=False,
    )
```

profile of v0, /device:TPU:1, one launch (start us, length us, event | category | flops | bytes accessed | tf_op | source)
XLA Modules:
  0.0 226.1 jit_solution(3943468472371128695)
XLA Ops:
  7.2 0.0 all-gather.4.cloned.1.call-start
  7.2 1.2 copy.29
  8.4 20.0 %all_to_all.38 = bf16[24,16,1024]{2,0,1:T(8,128)(2,1)} all-to-all(bf16[24,16,1024]{2,0,1:T(8,128)(2,1)S(1)} %bitcast.31), channel_id=1, replica_groups=mesh['row'=16,'col'=8] {'row'}, dimensions={1} | all-to-all | bytes 1572864 | tf_op jit(solution)/shard_map/all_to_all | solution.py:18
  28.4 0.0 all-gather.4.cloned.1.call-update
  28.5 0.0 all-gather.6.cloned.1.call-start
  28.5 1.2 copy.28
  29.7 22.4 %all_to_all.39 = bf16[24,8,2048]{2,0,1:T(8,128)(2,1)} all-to-all(bf16[24,8,2048]{2,0,1:T(8,128)(2,1)S(1)} %bitcast.32), channel_id=1, replica_groups=mesh['row'=16,'col'=8] {'col'}, dimensions={1} | all-to-all | bytes 1572864 | tf_op jit(solution)/shard_map/all_to_all | solution.py:26
  52.1 0.0 all-gather.6.cloned.1.call-update
  52.1 1.2 dynamic-slice
  54.0 0.8 add_dynamic-update-slice_fusion
  54.8 10.8 %all-reduce = s32[384]{0:T(512)S(1)} all-reduce(s32[384]{0:T(512)S(1)} %add_dynamic-update-slice_fusion), channel_id=1, replica_groups=mesh['row'=16,'col'=8] {'row'}, use_global_device_ids=true, to_apply=%add | all-reduce | flops 384 | bytes 3072
  65.6 26.1 %all-gather = s32[8,1,384]{2,1,0:T(1,128)S(1)} all-gather(s32[1,1,384]{2,1,0:T(1,128)S(1)} %reshape.30), channel_id=1, replica_groups=mesh['row'=16,'col'=8] {'col'}, dimensions={0}, use_global_device_ids=true | all-gather | bytes 13824 | tf_op jit(solution)/shard_map/all_gather | solution.py:21
  91.7 1.4 convert_reduce_fusion.2
  93.1 28.6 %all-gather.4.cloned.1.call-done = bf16[3072,1024]{1,0:T(8,128)(2,1)} async-done(((bf16[384,1024]{1,0:T(8,128)(2,1)}), bf16[3072,1024]{1,0:T(8,128)(2,1)}) %all-gather.4.cloned.1.call-update) | async-done | bytes 6291472 | tf_op jit(solution)/shard_map/all_gather | solution.py:20
  121.7 3.7 %convert_reduce_fusion.1 = f32[1024]{0:T(1024)S(1)} fusion(bf16[3072,1024]{1,0:T(8,128)(2,1)} %all-gather.4.cloned.1.call-done), kind=kLoop, calls=%fused_computation.3 | loop fusion | flops 6290432 | bytes 6295552 | tf_op jit(solution)/shard_map/reduce_sum | solution.py:30
  125.4 0.1 dynamic_slice.7
  125.5 2.8 %fusion.7 = f32[128,128]{1,0:T(8,128)} fusion(bf16[3072,1024]{1,0:T(8,128)(2,1)} %all-gather.4.cloned.1.call-done, s32[]{:T(128)S(6)} %select_n.4, s32[3072]{0:T(1024)S(1)} %bitcast.34, f32[128]{0:T(128)S(1)} %dynamic_slice.7, f32[128]{0:T(128)S(1)} %convert_reduce_fusion.2), kind=kOutput, calls=%fused_computation.10 | convolution fusion | flops 101105664 | bytes 865284 | tf_op jit(solution)/shard_map/dot_general | solution.py:40
  128.4 65.5 %all-gather.6.cloned.1.call-done = bf16[3072,2048]{1,0:T(8,128)(2,1)} async-done(((bf16[192,2048]{1,0:T(8,128)(2,1)}), bf16[3072,2048]{1,0:T(8,128)(2,1)}) %all-gather.6.cloned.1.call-update) | async-done | bytes 12582928 | tf_op jit(solution)/shard_map/all_gather | solution.py:27
  193.9 6.5 %convert_reduce_fusion = f32[2048]{0:T(1024)S(1)} fusion(bf16[3072,2048]{1,0:T(8,128)(2,1)} %all-gather.6.cloned.1.call-done), kind=kLoop, calls=%fused_computation | loop fusion | flops 12580864 | bytes 12591104 | tf_op jit(solution)/shard_map/reduce_sum | solution.py:31
  200.4 18.9 %fusion.2 = f32[1024,2048]{1,0:T(8,128)} fusion(bf16[8,16,24,1024]{3,2,1,0:T(8,128)(2,1)} %bitcast.26, bf16[16,8,24,2048]{3,2,1,0:T(8,128)(2,1)} %bitcast.25, f32[2048]{0:T(1024)S(1)} %broadcast_multiply_fusion, f32[1024]{0:T(1024)S(1)} %broadcast_multiply_fusion.1), kind=kOutput, calls=%fused_computation.5 | convolution fusion | flops 12891193344 | bytes 27275264 | tf_op jit(solution)/shard_map/abtf,batg->fg/dot_general | solution.py:29
  (4 shorter events, 0.0 us)
Async XLA Ops:
  7.2 114.5 %all-gather.4.cloned.1.call-start = ((), (), s32[]{:S(2)}) async-start(), calls=%async_computation.2 | async-start | bytes 7077888 | tf_op jit(solution)/shard_map/all_gather | solution.py:20
  28.5 165.4 %all-gather.6.cloned.1.call-start = ((), (), s32[]{:S(2)}) async-start(), calls=%async_computation.3 | async-start | bytes 13369344 | tf_op jit(solution)/shard_map/all_gather | solution.py:27
Sparse Core Ops, SparseCore 0:
  28.6 93.0 all-gather.3
  123.4 70.4 all-gather.5
where the time goes:
time: 227 us; the launch traced here: 226 us
  waiting for transfers between devices  94.2 us (41%)
  blocking collectives  79.3 us (35%)
  matrix products  21.8 us (10%)
  between operations  14.7 us (6%)
  other arithmetic  12.3 us (5%)
  local copies, waits for them, and re-layouts  3.72 us (2%)
    all_gather x1, waiting for transfers between devices, shards(): col_panel = lax.all_gather(col_piece, 'row', axis=0, tiled=True)  65.5 us
    all_gather x1, waiting for transfers between devices, shards(): lax.all_gather(row_piece, 'col', axis=0, tiled=True)  28.6 us
    all_gather x1, blocking collectives, shards(): lax.all_gather(codes_rows, 'col', axis=0, tiled=True)  26.1 us
    all_to_all x1, blocking collectives, shards(): lax.all_to_all(activations, 'col', split_axis=1, concat_axis=0, tiled=True)  22.4 us
    all_to_all x1, blocking collectives, shards(): lax.all_to_all(activations, 'row', split_axis=1, concat_axis=0, tiled=True)  20 us
    dot_general x1, matrix products, shards(): jnp.einsum('abtf,batg->fg', row_view, col_view, preferred_element_type=jn...  18.9 us
    unnamed x1, blocking collectives  10.8 us
    reduce_sum x1, other arithmetic, shards(): mean_col = jnp.sum(col_panel, axis=0, dtype=jnp.float32) / total  6.45 us
  transfers between devices with their start and end apart: 2, of which 2 were waited for; matrix products, arithmetic and copies ran while one was open for 5% of the time, Pallas kernels for 0%

commit v1 on v0

--- a/solution.py
+++ b/solution.py
@@ -5,6 +5,12 @@
 
 TENANTS = 64
 LABELS = 2
+
+
+def swap_blocks(array, axis, split, join):
+    pieces = jnp.split(array, lax.axis_size(axis), axis=split)
+    received = lax.all_to_all(jnp.stack(pieces), axis, 0, 0)
+    return jnp.concatenate(received, axis=join)
 
 
 def shards(activations, tenant_ids, concept_labels):
@@ -23,7 +29,7 @@
     total = row_panel.shape[0]
     row_width = row_panel.shape[1]
     row_view = row_panel.reshape(col_count, row_count, local_tokens, row_width)
-    col_piece = lax.all_to_all(activations, "col", split_axis=1, concat_axis=0, tiled=True)
+    col_piece = swap_blocks(activations, "col", 1, 0)
     col_panel = lax.all_gather(col_piece, "row", axis=0, tiled=True)
     col_view = col_panel.reshape(row_count, col_count, local_tokens, col_panel.shape[1])
     gram = jnp.einsum("abtf,batg->fg", row_view, col_view, preferred_element_type=jnp.float32)

time: 227 us -> 240 us (1.057)
  local copies, waits for them, and re-layouts: 3.72 us -> 18.8 us
  waiting for transfers between devices: 94.2 us -> 91.7 us
    unnamed x3 -> x11, local copies, waits for them, and re-layouts: 1.25 us -> 16.7 us
    all_to_all x1, blocking collectives: 22.4 us -> 25 us  [swap_blocks(): received = lax.all_to_all(jnp.stack(pieces), axis, 0, 0)]
    all_gather x1, waiting for transfers between devices: 28.6 us -> 26.1 us  [shards(): lax.all_gather(row_piece, 'col', axis=0, tiled=True)]
  transfers between devices with their start and end apart: 2 -> 2, of which waited for: 2 -> 2; matrix products, arithmetic and copies ran while one was open for 5% -> 7% of each run, Pallas kernels for 0% -> 0%
where the time goes in v1:
time: 240 us
  waiting for transfers between devices  91.7 us (38%)
  blocking collectives  80.2 us (33%)
  matrix products  21.7 us (9%)
  local copies, waits for them, and re-layouts  18.8 us (8%)
  between operations  14.7 us (6%)
  other arithmetic  12.3 us (5%)
    all_gather x1, waiting for transfers between devices, shards(): col_panel = lax.all_gather(col_piece, 'row', axis=0, tiled=True)  65.5 us
    all_gather x1, waiting for transfers between devices, shards(): lax.all_gather(row_piece, 'col', axis=0, tiled=True)  26.1 us
    all_gather x1, blocking collectives, shards(): lax.all_gather(codes_rows, 'col', axis=0, tiled=True)  26.1 us
    all_to_all x1, blocking collectives, swap_blocks(): received = lax.all_to_all(jnp.stack(pieces), axis, 0, 0)  25 us
    all_to_all x1, blocking collectives, shards(): lax.all_to_all(activations, 'row', split_axis=1, concat_axis=0, tiled=True)  20 us
    dot_general x1, matrix products, shards(): jnp.einsum('abtf,batg->fg', row_view, col_view, preferred_element_type=jn...  18.8 us
    unnamed x11, local copies, waits for them, and re-layouts  16.7 us
    unnamed x1, blocking collectives  9.1 us
  transfers between devices with their start and end apart: 2, of which 2 were waited for; matrix products, arithmetic and copies ran while one was open for 7% of the time, Pallas kernels for 0%

profile of v1, /device:TPU:1, one launch (start us, length us, event | category | flops | bytes accessed | tf_op | source)
XLA Modules:
  0.0 239.6 jit_solution(7325707023849125161)
XLA Ops:
  7.2 0.0 all-gather.6.cloned.1.call-start
  7.2 1.2 copy.25
  8.4 20.0 %all_to_all.24 = bf16[24,16,1024]{2,0,1:T(8,128)(2,1)} all-to-all(bf16[24,16,1024]{2,0,1:T(8,128)(2,1)S(1)} %bitcast.46), channel_id=1, replica_groups=mesh['row'=16,'col'=8] {'row'}, dimensions={1} | all-to-all | bytes 1572864 | tf_op jit(solution)/shard_map/all_to_all | solution.py:24
  28.4 0.0 all-gather.6.cloned.1.call-update
  28.5 0.0 all-gather.4.cloned.1.call-start
  28.5 0.9 bitcast_dynamic-update-slice_fusion.7
  29.4 0.9 bitcast_dynamic-update-slice_fusion.6
  30.3 0.9 bitcast_dynamic-update-slice_fusion.5
  31.2 0.9 bitcast_dynamic-update-slice_fusion.4
  32.1 0.9 bitcast_dynamic-update-slice_fusion.3
  33.0 0.9 bitcast_dynamic-update-slice_fusion.2
  33.9 0.9 bitcast_dynamic-update-slice_fusion.1
  34.8 0.9 bitcast_dynamic-update-slice_fusion
  35.7 25.0 %all_to_all.25 = bf16[8,24,2048]{2,1,0:T(8,128)(2,1)} all-to-all(bf16[8,24,2048]{2,1,0:T(8,128)(2,1)S(1)} %bitcast_dynamic-update-slice_fusion), channel_id=1, replica_groups=mesh['row'=16,'col'=8] {'col'}, dimensions={0} | all-to-all | bytes 1572864 | tf_op jit(solution)/shard_map/all_to_all | solution.py:12
  60.7 0.0 all-gather.4.cloned.1.call-update
  60.8 1.2 dynamic-slice
  62.7 0.8 add_dynamic-update-slice_fusion
  63.4 9.1 %all-reduce = s32[384]{0:T(512)S(1)} all-reduce(s32[384]{0:T(512)S(1)} %add_dynamic-update-slice_fusion), channel_id=1, replica_groups=mesh['row'=16,'col'=8] {'row'}, use_global_device_ids=true, to_apply=%add | all-reduce | flops 384 | bytes 3072
  72.6 26.1 %all-gather = s32[8,1,384]{2,1,0:T(1,128)S(1)} all-gather(s32[1,1,384]{2,1,0:T(1,128)S(1)} %reshape.31), channel_id=1, replica_groups=mesh['row'=16,'col'=8] {'col'}, dimensions={0}, use_global_device_ids=true | all-gather | bytes 13824 | tf_op jit(solution)/shard_map/all_gather | solution.py:27
  98.6 1.4 convert_reduce_fusion.2
  100.0 26.1 %all-gather.6.cloned.1.call-done = bf16[3072,1024]{1,0:T(8,128)(2,1)} async-done(((bf16[384,1024]{1,0:T(8,128)(2,1)}), bf16[3072,1024]{1,0:T(8,128)(2,1)}) %all-gather.6.cloned.1.call-update) | async-done | bytes 6291472 | tf_op jit(solution)/shard_map/all_gather | solution.py:26
  126.1 3.7 %convert_reduce_fusion.1 = f32[1024]{0:T(1024)S(1)} fusion(bf16[3072,1024]{1,0:T(8,128)(2,1)} %all-gather.6.cloned.1.call-done), kind=kLoop, calls=%fused_computation.3 | loop fusion | flops 6290432 | bytes 6295552 | tf_op jit(solution)/shard_map/reduce_sum | solution.py:36
  129.8 0.1 dynamic_slice.7
  129.9 2.8 %fusion.8 = f32[128,128]{1,0:T(8,128)} fusion(bf16[3072,1024]{1,0:T(8,128)(2,1)} %all-gather.6.cloned.1.call-done, s32[]{:T(128)S(6)} %select_n.4, s32[3072]{0:T(1024)S(1)} %bitcast.48, f32[128]{0:T(128)S(1)} %dynamic_slice.7, f32[128]{0:T(128)S(1)} %convert_reduce_fusion.2), kind=kOutput, calls=%fused_computation.11 | convolution fusion | flops 101105664 | bytes 865284 | tf_op jit(solution)/shard_map/dot_general | solution.py:46
  132.7 65.5 %all-gather.4.cloned.1.call-done = bf16[3072,2048]{1,0:T(8,128)(2,1)} async-done(((bf16[192,2048]{1,0:T(8,128)(2,1)}), bf16[3072,2048]{1,0:T(8,128)(2,1)}) %all-gather.4.cloned.1.call-update) | async-done | bytes 12582928 | tf_op jit(solution)/shard_map/all_gather | solution.py:33
  198.3 6.5 %convert_reduce_fusion = f32[2048]{0:T(1024)S(1)} fusion(bf16[3072,2048]{1,0:T(8,128)(2,1)} %all-gather.4.cloned.1.call-done), kind=kLoop, calls=%fused_computation | loop fusion | flops 12580864 | bytes 12591104 | tf_op jit(solution)/shard_map/reduce_sum | solution.py:37
  204.8 18.8 %fusion.3 = f32[1024,2048]{0,1:T(8,128)} fusion(bf16[8,16,24,1024]{3,2,1,0:T(8,128)(2,1)} %bitcast.42, bf16[16,8,24,2048]{3,2,1,0:T(8,128)(2,1)} %bitcast.41, f32[2048]{0:T(1024)S(1)} %broadcast_multiply_fusion, f32[1024]{0:T(1024)S(1)} %broadcast_multiply_fusion.1), kind=kOutput, calls=%fused_computation.6 | convolution fusion | flops 12891193344 | bytes 27275264 | tf_op jit(solution)/shard_map/abtf,batg->fg/dot_general | solution.py:35
  223.6 9.1 %copy.17 = f32[1024,2048]{1,0:T(8,128)} copy(f32[1024,2048]{0,1:T(8,128)} %fusion.3) | data formatting | bytes 16777216
  (4 shorter events, 0.0 us)
Async XLA Ops:
  7.2 118.9 %all-gather.6.cloned.1.call-start = ((), (), s32[]{:S(2)}) async-start(), calls=%async_computation.3 | async-start | bytes 7077888 | tf_op jit(solution)/shard_map/all_gather | solution.py:26
  28.5 169.8 %all-gather.4.cloned.1.call-start = ((), (), s32[]{:S(2)}) async-start(), calls=%async_computation.2 | async-start | bytes 13369344 | tf_op jit(solution)/shard_map/all_gather | solution.py:33
Sparse Core Ops, SparseCore 0:
  28.6 97.4 all-gather.5
  127.8 70.4 all-gather.3
